TPU v7x, 512 devices: a whole 4x8x8 slice. The times are simulated.
512 devices in a mesh: rep: 64 (over z, y_lo, core), voc: 8 (over y_hi, x).
Axes of the slice: x: 4, y: 8 (y_hi: 2, y_lo: 4; y = y_hi * 4 + y_lo), z: 8, core: 2. Of those that a mesh axis runs over, the one named last changes fastest.
Arguments:
- states: bfloat16 [2, 256, 24576], P(None, None, 'rep'), may hold values from -6 to 6
- head_weight: bfloat16 [24576, 16384], P('rep', 'voc'), may hold values from -0.21875 to 0.21875
- pair_order: int32 [2, 32], replicated, may hold values from 0 to 31, each once within a row
- row_example: int32 [2, 32, 256], replicated, may hold values from 0 to 255, each once within a row
Outputs:
- state_grad: bfloat16 [2, 256, 24576], P(None, None, 'rep')
- head_grad: bfloat16 [24576, 16384], P('rep', 'voc')
Inputs may be any that keep to these rules, and one draw needn't show every extreme that they name: Each row pair_order[m] holds every replica once. Each row row_example[m, r] holds every number of 0 to 255 once.
All inputs are finite; a program needn't handle non-finite values.
Results may differ from a plain program's by a relative error of at most 0.0055.
Values may be sent and summed in bfloat16 or wider, within the bound.
A program may use at most 64 MiB of HBM per device.

v0:
```python
import jax
import jax.numpy as jnp
from jax import lax
from jax.sharding import PartitionSpec as P

distill_weight = 0.0625


def partner_2(block, axis, apart):
    count = lax.axis_size(axis)
    route = []
    for low in range(count):
        high = low | 1 << apart
        if high != low and high < count:
            route += [(low, high), (high, low)]
    return lax.ppermute(block, axis, route)


def partner_table(pair_order):
    slot_count = pair_order.shape[1]
    slot_ids = jnp.arange(slot_count, dtype=jnp.int32)
    matches = pair_order[:, None, :] == slot_ids[None, :, None]
    position = jnp.sum(jnp.where(matches, slot_ids[None, None, :], 0), axis=2)
    following = (position + 1) % slot_count
    return jnp.take_along_axis(pair_order, following, axis=1)


def to_examples(rows_in, examples):
    slot_count = examples.shape[1]
    slot_ids = jnp.arange(slot_count, dtype=jnp.int32)
    onehot = (examples[:, None, :] == slot_ids[None, :, None]).astype(jnp.bfloat16)
    return jnp.einsum("mei,miw->mew", onehot, rows_in, preferred_element_type=jnp.float32).astype(
        jnp.bfloat16
    )


def differences(received, pair_table):
    partner_rows = jax.vmap(
        lambda source_block, index_row: jnp.take(source_block, index_row, axis=0)
    )(received, pair_table)
    spread = received.astype(jnp.float32) - partner_rows.astype(jnp.float32)
    return (distill_weight * spread).astype(jnp.bfloat16)


def body(states, head_weight, pair_order, row_example):
    micro_count, row_count, half_width = states.shape
    vocab_shard = head_weight.shape[1]
    devices = lax.axis_size("rep")
    rep_place = lax.axis_index("rep")
    replica = rep_place // 2
    pair_side = rep_place % 2
    examples = lax.dynamic_index_in_dim(row_example, replica, 1, keepdims=False)
    ordered = to_examples(states, examples)
    flat_states = ordered.reshape(micro_count * row_count, half_width)
    partial_logits = jnp.dot(flat_states, head_weight, preferred_element_type=jnp.float32)
    partial_logits = partial_logits.reshape(micro_count, row_count, vocab_shard)
    partner = partner_table(pair_order)
    sources = jnp.arange(devices, dtype=jnp.int32)
    partner_dev = 2 * jnp.take(partner, sources // 2, axis=1) + sources % 2
    row_span = row_count // 2
    own_rows = lax.dynamic_slice_in_dim(partial_logits, pair_side * row_span, row_span, 1)
    theirs = lax.dynamic_slice_in_dim(partial_logits, (1 - pair_side) * row_span, row_span, 1)
    logits = (own_rows + partner_2(theirs, "rep", 0)).astype(jnp.bfloat16)
    logit_tiles = logits.reshape(micro_count, devices, row_span // devices, vocab_shard)
    graded = lax.all_to_all(
        differences(
            lax.all_to_all(logit_tiles, "rep", split_axis=1, concat_axis=1, tiled=True), partner_dev
        ),
        "rep",
        split_axis=1,
        concat_axis=1,
        tiled=True,
    )
    graded = graded.reshape(micro_count, row_span, vocab_shard)
    other_half = partner_2(graded, "rep", 0)
    first_rows = jnp.where(pair_side == 0, graded, other_half)
    second_rows = jnp.where(pair_side == 0, other_half, graded)
    gradient = jnp.concatenate([first_rows, second_rows], axis=1)
    flat_grad = gradient.reshape(micro_count * row_count, vocab_shard)
    head_grad = jnp.einsum(
        "rw,rv->wv", flat_states, flat_grad, preferred_element_type=jnp.float32
    ).astype(jnp.bfloat16)
    local_state = jnp.einsum(
        "rv,wv->rw", flat_grad, head_weight, preferred_element_type=jnp.float32
    )
    state_canon = lax.psum(local_state, "voc").astype(jnp.bfloat16)
    state_canon = state_canon.reshape(micro_count, row_count, half_width)
    state_grad = jnp.take_along_axis(state_canon, examples[:, :, None], axis=1)
    return (state_grad, head_grad)


def solution(mesh):
    return jax.shard_map(
        body,
        mesh=mesh,
        in_specs=(P(None, None, "rep"), P("rep", "voc"), P(), P()),
        out_specs=(P(None, None, "rep"), P("rep", "voc")),
        check_vma=False,
    )
```

profile of v0, /device:TPU:80, one launch (start us, length us, event | category | flops | bytes accessed | tf_op | source)
XLA Modules:
  0.0 188.6 jit_solution(7143207101017817800)
XLA Ops:
  0.6 0.0 copy-start
  0.7 0.8 fusion.6
  1.5 1.3 convolution_convert_fusion
  2.9 0.0 copy-done
  2.9 3.2 %fusion = f32[2,256,2048]{2,1,0:T(8,128)} fusion(bf16[2,256,384]{2,1,0:T(8,128)(2,1)S(1)} %convolution_convert_fusion, bf16[384,2048]{1,0:T(8,128)(2,1)S(1)} %copy-done), kind=kOutput, calls=%fused_computation.9 | convolution fusion | flops 805306368 | bytes 6160384 | tf_op jit(solution)/shard_map/dot_general | solution.py:55
  6.1 3.2 %constant_dynamic-slice_fusion = f32[2,128,2048]{2,1,0:T(8,128)} fusion(f32[2,256,2048]{2,1,0:T(8,128)} %fusion, s32[]{:T(128)S(6)} %select_n.181), kind=kLoop, calls=%fused_computation.66 | loop fusion | bytes 4194308 | tf_op jit(solution)/shard_map/dynamic_slice | solution.py:62
  9.2 1.9 %collective-permute-start = (f32[2,128,2048]{2,1,0:T(8,128)}, f32[2,128,2048]{2,1,0:T(8,128)}, u32[]{:S(2)}, u32[]{:S(2)}) collective-permute-start(f32[2,128,2048]{2,1,0:T(8,128)} %constant_dynamic-slice_fusion), channel_id=1, source_target_pairs={{0,8},{8,0},{16,24},{24,16},{32,40},{40,32},{48,56},{56,48},{64,72... | collective-permute-start | bytes 6291464 | tf_op jit(solution)/shard_map/ppermute | solution.py:16
  11.2 4.5 %collective-permute-done = f32[2,128,2048]{2,1,0:T(8,128)} collective-permute-done((f32[2,128,2048]{2,1,0:T(8,128)}, f32[2,128,2048]{2,1,0:T(8,128)}, u32[]{:S(2)}, u32[]{:S(2)}) %collective-permute-start) | collective-permute-done | bytes 2097184 | tf_op jit(solution)/shard_map/ppermute | solution.py:16
  15.6 3.5 %add_convert_fusion = bf16[2,128,2048]{2,1,0:T(8,128)(2,1)} fusion(f32[2,128,2048]{2,1,0:T(8,128)} %collective-permute-done, f32[2,256,2048]{2,1,0:T(8,128)} %fusion, s32[]{:T(128)S(6)} %select_n.180), kind=kLoop, calls=%fused_computation.7 | loop fusion | flops 1048576 | bytes 5242884 | tf_op jit(solution)/shard_map/convert_element_type | solution.py:63
  19.1 1.7 reshape.256
  20.8 0.0 copy-start.1
  20.8 2.2 %copy.31 = bf16[2,64,2,2048]{3,2,0,1:T(2,128)(2,1)} copy(bf16[2,64,2,2048]{3,2,1,0:T(2,128)(2,1)S(1)} %reshape.256) | data formatting | bytes 2097152 | tf_op jit(solution)/shard_map/reshape | solution.py:64
  23.0 13.3 %all-to-all-start = ((bf16[2,64,2,2048]{3,2,0,1:T(2,128)(2,1)}), bf16[2,64,2,2048]{3,2,0,1:T(2,128)(2,1)S(1)}, u32[]{:S(2)}, u32[]{:S(2)}) async-start(bf16[2,64,2,2048]{3,2,0,1:T(2,128)(2,1)} %copy.31), calls=%async_computation | async-start | bytes 2097152 | tf_op jit(solution)/shard_map/all_to_all | solution.py:67
  36.4 0.0 copy-done.1
  36.4 0.1 select_reduce_fusion
  36.5 0.1 copy.32
  36.6 0.1 copy.33
  36.7 0.1 reshape.268
  36.8 0.9 gather_fusion.1
  37.7 0.1 reshape.271
  37.8 0.1 copy.34
  37.9 0.6 gather_fusion
  38.5 0.1 copy.35
  38.6 0.1 reshape.274
  38.7 0.1 copy.36
  38.8 25.5 %all-to-all-done = bf16[2,64,2,2048]{3,2,0,1:T(2,128)(2,1)S(1)} async-done(((bf16[2,64,2,2048]{3,2,0,1:T(2,128)(2,1)}), bf16[2,64,2,2048]{3,2,0,1:T(2,128)(2,1)S(1)}, u32[]{:S(2)}, u32[]{:S(2)}) %all-to-all-start) | async-done | bytes 1048608 | tf_op jit(solution)/shard_map/all_to_all | solution.py:67
  64.3 3.7 %gather_fusion.2 = bf16[128,2,2048]{2,1,0:T(2,128)(2,1)} fusion(bf16[2,64,2,2048]{3,2,0,1:T(2,128)(2,1)S(1)} %all-to-all-done, s32[128]{0:T(128)S(1)} %reshape.274), kind=kCustom, calls=%fused_computation.2 | custom fusion | bytes 2098176 | tf_op jit(solution)/shard_map/vmap(jit(_take))/gather | solution.py:39
  68.0 3.5 %multiply_convert_fusion = bf16[2,64,2,2048]{3,2,0,1:T(2,128)(2,1)S(1)} fusion(bf16[2,64,2,2048]{3,2,0,1:T(2,128)(2,1)S(1)} %all-to-all-done, pred[2,64]{0,1:T(8,128)(4,1)S(1)} %copy.36, bf16[2,64,2,2048]{3,2,1,0:T(2,128)(2,1)} %bitcast.49), kind=kLoop, calls=%fused_computation.6 | loop fusion | flops 3145728 | bytes 3145856 | tf_op jit(solution)/shard_map/convert_element_type | solution.py:42
  71.6 34.4 %all_to_all.10 = bf16[2,64,2,2048]{3,2,0,1:T(2,128)(2,1)S(1)} all-to-all(bf16[2,64,2,2048]{3,2,0,1:T(2,128)(2,1)S(1)} %multiply_convert_fusion), channel_id=1, replica_groups=mesh['rep'=64,'voc'=8] {'rep'}, dimensions={1} | all-to-all | bytes 2097152 | tf_op jit(solution)/shard_map/all_to_all | solution.py:65
  105.9 1.7 copy.38
  107.6 1.5 reshape.257
  109.1 2.1 %collective-permute-start.1 = (bf16[2,128,2048]{2,1,0:T(8,128)(2,1)S(1)}, bf16[2,128,2048]{2,1,0:T(8,128)(2,1)}, u32[]{:S(2)}, u32[]{:S(2)}) collective-permute-start(bf16[2,128,2048]{2,1,0:T(8,128)(2,1)S(1)} %reshape.257), channel_id=1, source_target_pairs={{0,8},{8,0},{16,24},{24,16},{32,40},{40,32},{48,56},{56,48},{64,72... | collective-permute-start | bytes 3145736 | tf_op jit(solution)/shard_map/ppermute | solution.py:16
  111.2 2.6 %collective-permute-done.1 = bf16[2,128,2048]{2,1,0:T(8,128)(2,1)} collective-permute-done((bf16[2,128,2048]{2,1,0:T(8,128)(2,1)S(1)}, bf16[2,128,2048]{2,1,0:T(8,128)(2,1)}, u32[]{:S(2)}, u32[]{:S(2)}) %collective-permute-start.1) | collective-permute-done | bytes 1048608 | tf_op jit(solution)/shard_map/ppermute | solution.py:16
  113.8 1.4 broadcast_select_fusion.2
  115.2 2.2 %bitcast_convert_fusion = bf16[384,2048]{1,0:T(8,128)(2,1)} fusion(bf16[2,256,384]{2,1,0:T(8,128)(2,1)S(1)} %convolution_convert_fusion, bf16[2,128,2048]{2,1,0:T(8,128)(2,1)S(1)} %get-tuple-element.5, bf16[2,128,2048]{2,1,0:T(8,128)(2,1)S(1)} %get-tuple-element.4), kind=kOutput, calls=%fused_computation.4 | convolution fusion | flops 810287104 | bytes 4063232 | tf_op jit(solution)/shard_map/rw,rv->wv/dot_general | solution.py:80
  117.3 0.2 pad_maximum_fusion
  117.6 1.3 fusion.19
  118.9 65.2 %all-reduce.1 = bf16[512,384]{1,0:T(8,128)(2,1)S(1)} all-reduce(f32[512,384]{1,0:T(8,128)S(1)} %fusion.19), channel_id=1, replica_groups=mesh['rep'=64,'voc'=8] {'voc'}, use_global_device_ids=true, to_apply=%region_1.2 | all-reduce | flops 196608 | bytes 1179648 | tf_op jit(solution)/shard_map/psum | solution.py:86
  184.1 3.7 %gather_fusion.3 = bf16[512,384]{1,0:T(8,128)(2,1)S(1)} fusion(bf16[2,256,384]{2,1,0:T(8,128)(2,1)S(1)} %bitcast.48, s32[512]{0:T(512)S(1)} %bitcast.47), kind=kCustom, calls=%fused_computation.3 | custom fusion | bytes 790528 | tf_op jit(solution)/shard_map/jit(take_along_axis)/gather | solution.py:88
  187.7 0.9 broadcast_select_fusion.3
  (11 shorter events, 0.1 us)
Async XLA Ops:
  0.6 2.2 %copy-start = (bf16[384,2048]{1,0:T(8,128)(2,1)S(1)}, bf16[384,2048]{1,0:T(8,128)(2,1)}, u32[]{:S(2)}) copy-start(bf16[384,2048]{1,0:T(8,128)(2,1)} %param.5) | copy-start | bytes 4718596
  9.2 6.4 %collective-permute-start = (f32[2,128,2048]{2,1,0:T(8,128)}, f32[2,128,2048]{2,1,0:T(8,128)}, u32[]{:S(2)}, u32[]{:S(2)}) collective-permute-start(f32[2,128,2048]{2,1,0:T(8,128)} %constant_dynamic-slice_fusion), channel_id=1, source_target_pairs={{0,8},{8,0},{16,24},{24,16},{32,40},{40,32},{48,56},{56,48},{64,72... | collective-permute-start | bytes 6291464 | tf_op jit(solution)/shard_map/ppermute | solution.py:16
  20.8 15.6 %copy-start.1 = (s32[2,32]{1,0:T(2,128)S(1)}, s32[2,32]{1,0:T(2,128)}, u32[]{:S(2)}) copy-start(s32[2,32]{1,0:T(2,128)} %param.6) | copy-start | bytes 772
  23.0 41.3 %all-to-all-start = ((bf16[2,64,2,2048]{3,2,0,1:T(2,128)(2,1)}), bf16[2,64,2,2048]{3,2,0,1:T(2,128)(2,1)S(1)}, u32[]{:S(2)}, u32[]{:S(2)}) async-start(bf16[2,64,2,2048]{3,2,0,1:T(2,128)(2,1)} %copy.31), calls=%async_computation | async-start | bytes 2097152 | tf_op jit(solution)/shard_map/all_to_all | solution.py:67
  109.1 4.7 %collective-permute-start.1 = (bf16[2,128,2048]{2,1,0:T(8,128)(2,1)S(1)}, bf16[2,128,2048]{2,1,0:T(8,128)(2,1)}, u32[]{:S(2)}, u32[]{:S(2)}) collective-permute-start(bf16[2,128,2048]{2,1,0:T(8,128)(2,1)S(1)} %reshape.257), channel_id=1, source_target_pairs={{0,8},{8,0},{16,24},{24,16},{32,40},{40,32},{48,56},{56,48},{64,72... | collective-permute-start | bytes 3145736 | tf_op jit(solution)/shard_map/ppermute | solution.py:16
where the time goes:
time: 189 us
  blocking collectives  99.6 us (53%)
  waiting for transfers between devices  32.5 us (17%)
  local copies, waits for them, and re-layouts  19.8 us (10%)
  starting transfers between devices  17.4 us (9%)
  other arithmetic  10.5 us (6%)
  matrix products  7.95 us (4%)
    psum x1, blocking collectives, body(): state_canon = lax.psum(local_state, 'voc').astype(jnp.bfloat16)  65.2 us
    all_to_all x1, blocking collectives, body(): lax.all_to_all(differences(lax.all_to_all(logit_tiles, 'rep', split_axis=...  34.4 us
    all_to_all x1, waiting for transfers between devices, body(): lax.all_to_all(logit_tiles, 'rep', split_axis=1, concat_axis=1, tiled=True)  25.5 us
    all_to_all x1, starting transfers between devices, body(): lax.all_to_all(logit_tiles, 'rep', split_axis=1, concat_axis=1, tiled=True)  13.3 us
    ppermute x2, waiting for transfers between devices, partner_2(): return lax.ppermute(block, axis, route)  7.02 us
    ppermute x2, starting transfers between devices, partner_2(): return lax.ppermute(block, axis, route)  4.01 us
    reshape x2, local copies, waits for them, and re-layouts, body(): logits.reshape(micro_count, devices, row_span // devices, vocab_shard)  3.95 us
    gather x2, local copies, waits for them, and re-layouts, differences(): jnp.take(source_block, index_row, axis=0)  3.79 us
  transfers between devices with their start and end apart: 3, of which 3 were waited for; matrix products, arithmetic and copies ran while one was open for 1% of the time, Pallas kernels for 0%

commit v1 on v0

v1 whole, which is shorter than its diff:
```python
import functools

import jax
import jax.numpy as jnp
from jax import lax
from jax.experimental import pallas as pl
from jax.experimental.pallas import tpu as pltpu
from jax.sharding import PartitionSpec as P

MESH = pl.DeviceIdType.MESH
SCALE = 0.0625
F32, BF16 = jnp.float32, jnp.bfloat16


def kernel(
    dims,
    pair_order,
    states_hbm,
    weight_hbm,
    example_hbm,
    state_hbm,
    head_hbm,
    weight,
    weight_t,
    states,
    examples,
    onehot,
    ordered,
    ordered_t,
    mine,
    sent,
    got,
    logits,
    pool_0,
    pool_1,
    spread,
    grad,
    part,
    part_b,
    xin,
    half,
    half_in,
    total,
    state_out,
    head_out,
    partner,
    in_sem,
    out_sem,
    pair_send,
    pair_recv,
    one_send,
    one_recv,
    two_send,
    two_recv,
    fwd_send,
    fwd_recv,
    xs_send,
    xs_recv,
    y_send,
    y_recv,
    xg_send,
    xg_recv,
):
    NZ, NY, NX, NH = dims
    pools = (pool_0, pool_1)
    mb, rows, width = states.shape
    vocab = weight.shape[1]
    count = NZ * NY
    side_rows = rows // 2
    chunk = side_rows // 2
    rg, cg = side_rows // NZ, vocab // NY
    zh = NZ // 2
    quarter = rows // NX

    rep, voc = lax.axis_index("rep"), lax.axis_index("voc")
    core = lax.rem(rep, 2)
    rid = rep // 2
    z, y = rid // NY, lax.rem(rid, NY)
    h, x = voc // NX, lax.rem(voc, NX)
    slot_of = lambda zz, yy: yy * NZ + lax.rem(zz, 2) * zh + zz // 2
    my_slot = slot_of(z, y)
    pair = {"rep": rid * 2 + 1 - core}
    across = {"voc": (NH - 1 - h) * NX + x}

    loads = [
        pltpu.make_async_copy(example_hbm, examples, in_sem.at[0]),
        pltpu.make_async_copy(states_hbm, states, in_sem.at[1]),
        pltpu.make_async_copy(weight_hbm, weight, in_sem.at[2]),
    ]
    for load in loads:
        load.start()

    barrier = pltpu.get_barrier_semaphore()

    @pl.loop(0, count)
    def _(k):
        @pl.when(k != rid)
        def _():
            pl.semaphore_signal(barrier, inc=1, device_id={"rep": k * 2 + core}, device_id_type=MESH)

    pl.semaphore_signal(barrier, inc=1, device_id=pair, device_id_type=MESH)
    for k in range(1, NX):
        pl.semaphore_signal(
            barrier, inc=1, device_id={"voc": h * NX + lax.rem(x + k, NX)}, device_id_type=MESH
        )
    if NH > 1:
        pl.semaphore_signal(barrier, inc=1, device_id=across, device_id_type=MESH)

    loads[0].wait()
    loads[1].wait()
    ids = lax.broadcasted_iota(jnp.int32, (rows, rows), 0)
    for m in range(mb):
        row = examples[m, pl.ds(rid, 1), :]
        onehot[m] = (ids == row).astype(BF16)
        ordered[m] = jnp.dot(onehot[m], states[m], preferred_element_type=F32).astype(BF16)
    loads[2].wait()

    def partials(side, target):
        at = pl.multiple_of(side * side_rows, side_rows)
        left = jnp.concatenate([ordered[m, pl.ds(at, side_rows), :] for m in range(mb)], axis=0)

        @pl.loop(0, NY)
        def _(j):
            cols = pl.ds(pl.multiple_of(j * cg, cg), cg)
            out = jnp.dot(left, weight[:, cols], preferred_element_type=F32)
            for m in range(mb):
                for u in range(2):
                    lo = m * side_rows + u * chunk
                    target[m, u, :, cols] = out[lo : lo + chunk]

    partials(1 - core, sent)
    pl.semaphore_wait(barrier, count - 1 + 1 + NX - 1 + (1 if NH > 1 else 0))

    def pair_copy(m, u):
        return pltpu.make_async_remote_copy(
            src_ref=sent.at[m, u],
            dst_ref=got.at[m, u],
            send_sem=pair_send.at[m, u],
            recv_sem=pair_recv.at[m, u],
            device_id=pair,
            device_id_type=MESH,
        )

    for m in range(mb):
        for u in range(2):
            pair_copy(m, u).start()
    partials(core, mine)

    for m in range(mb):
        for u in range(2):
            pair_copy(m, u).wait_recv()

            @pl.loop(0, NY)
            def _(j):
                cols = pl.ds(pl.multiple_of(j * cg, cg), cg)
                both = (mine[m, u, :, cols] + got[m, u, :, cols]).astype(BF16)
                logits[m, pl.ds(j * NZ + u * zh, zh)] = both.reshape(zh, rg, cg)

            @pl.loop(0, zh * NY)
            def _(k):
                zt = u + 2 * lax.rem(z // 2 + k // NY, zh)
                yt = lax.rem(y + lax.rem(k, NY), NY)
                target = zt * NY + yt
                src, dst = logits.at[m, slot_of(zt, yt)], pools[m].at[rid]

                @pl.when(target != rid)
                def _():
                    pltpu.make_async_remote_copy(
                        src_ref=src,
                        dst_ref=dst,
                        send_sem=one_send.at[m],
                        recv_sem=one_recv.at[m],
                        device_id={"rep": target * 2 + core},
                        device_id_type=MESH,
                    ).start()

                @pl.when(target == rid)
                def _():
                    pltpu.make_async_copy(src, dst, one_recv.at[m]).start()

    for m in range(mb):

        @pl.loop(0, count)
        def _(r):
            found = jnp.int32(0)
            for k in range(count):
                found += jnp.where(pair_order[m, k] == r, pair_order[m, (k + 1) % count], 0)
            partner[m, r] = found

        ordered_t[m] = ordered[m].T

    @pl.loop(0, NY)
    def _(j):
        at = pl.multiple_of(j * cg, cg)
        weight_t[pl.ds(at, cg), :] = weight[:, pl.ds(at, cg)].T

    for m in range(mb):
        pool = pools[m]
        pltpu.make_async_copy(pool, pool, one_recv.at[m]).wait()

        def place(k):
            return lax.rem(z + k // NY, NZ) * NY + lax.rem(y + lax.rem(k, NY), NY)

        @pl.loop(0, count // 4)
        def _(b):
            for i in range(4):
                r = place(b * 4 + i)
                own, other = pool[r], pool[partner[m, r]]
                spread[m, r] = (SCALE * (own.astype(F32) - other.astype(F32))).astype(BF16)
            for i in range(4):
                r = place(b * 4 + i)
                src, dst = spread.at[m, r], grad.at[m, core, my_slot]

                @pl.when(r != rid)
                def _():
                    pltpu.make_async_remote_copy(
                        src_ref=src,
                        dst_ref=dst,
                        send_sem=two_send.at[m],
                        recv_sem=two_recv.at[m],
                        device_id={"rep": r * 2 + core},
                        device_id_type=MESH,
                    ).start()

                @pl.when(r == rid)
                def _():
                    pltpu.make_async_copy(src, dst, two_recv.at[m]).start()

    def forward(m):
        return pltpu.make_async_remote_copy(
            src_ref=grad.at[m, core],
            dst_ref=grad.at[m, core],
            send_sem=fwd_send.at[m],
            recv_sem=fwd_recv.at[m],
            device_id=pair,
            device_id_type=MESH,
        )

    def scatter(m, k):
        xt = lax.rem(x + k, NX)
        return pltpu.make_async_remote_copy(
            src_ref=part_b.at[m, xt],
            dst_ref=xin.at[m, x],
            send_sem=xs_send.at[m],
            recv_sem=xs_recv.at[m],
            device_id={"voc": h * NX + xt},
            device_id_type=MESH,
        )

    def gather(m, k):
        xt = lax.rem(x + k, NX)
        return pltpu.make_async_remote_copy(
            src_ref=total.at[m, x],
            dst_ref=total.at[m, x],
            send_sem=xg_send.at[m],
            recv_sem=xg_recv.at[m],
            device_id={"voc": h * NX + xt},
            device_id_type=MESH,
        )

    def cross(m):
        return pltpu.make_async_remote_copy(
            src_ref=half.at[m],
            dst_ref=half_in.at[m],
            send_sem=y_send.at[m],
            recv_sem=y_recv.at[m],
            device_id=across,
            device_id_type=MESH,
        )

    def others(ref, sem):
        few = ref.at[pl.ds(0, NX - 1)]
        pltpu.make_async_copy(few, few, sem).wait()

    def block(m, j):
        return grad[m, :, pl.ds(j * NZ, NZ)].reshape(rows, cg)

    for m in range(mb):
        pltpu.make_async_copy(grad.at[m, core], grad.at[m, core], two_recv.at[m]).wait()
        forward(m).start()
        forward(m).wait_recv()

        part[m] = jnp.zeros((rows, width), F32)

        @pl.loop(0, NY)
        def _(j):
            at = pl.multiple_of(j * cg, cg)
            part[m] += jnp.dot(block(m, j), weight_t[pl.ds(at, cg), :], preferred_element_type=F32)

        part_b[m] = part[m].astype(BF16).reshape(NX, quarter, width)
        for k in range(1, NX):
            scatter(m, k).start()
        if m == mb - 1:
            for j in range(NY):
                cols = pl.ds(j * cg, cg)
                out = jnp.dot(ordered_t[0], block(0, j), preferred_element_type=F32)
                for n in range(1, mb):
                    out += jnp.dot(ordered_t[n], block(n, j), preferred_element_type=F32)
                head_out[:, cols] = out.astype(BF16)
                pltpu.make_async_copy(head_out.at[:, cols], head_hbm.at[:, cols], out_sem.at[0]).start()

        others(xin.at[m], xs_recv.at[m])
        acc = part[m, pl.ds(pl.multiple_of(x * quarter, quarter), quarter), :]
        for k in range(1, NX):
            acc += xin[m, lax.rem(x + k, NX)].astype(F32)
        half[m] = acc.astype(BF16)
        if NH > 1:
            cross(m).start()
            cross(m).wait_recv()
            total[m, x] = (half[m].astype(F32) + half_in[m].astype(F32)).astype(BF16)
        else:
            total[m, x] = half[m]
        for k in range(1, NX):
            gather(m, k).start()
        others(total.at[m], xg_recv.at[m])
        state_out[m] = lax.dot_general(
            onehot[m],
            total[m].reshape(rows, width),
            (((0,), (0,)), ((), ())),
            preferred_element_type=F32,
        ).astype(BF16)
        pltpu.make_async_copy(state_out.at[m], state_hbm.at[m], out_sem.at[1]).start()

    most = logits.at[0, pl.ds(0, count - 1)]
    for m in range(mb):
        for u in range(2):
            pair_copy(m, u).wait_send()
        pltpu.make_async_copy(most, most, one_send.at[m]).wait()
        pltpu.make_async_copy(most, most, two_send.at[m]).wait()
        forward(m).wait_send()
        others(part_b.at[m], xs_send.at[m])
        others(total.at[m], xg_send.at[m])
        if NH > 1:
            cross(m).wait_send()
    pltpu.make_async_copy(head_out, head_hbm, out_sem.at[0]).wait()
    pltpu.make_async_copy(state_out, state_hbm, out_sem.at[1]).wait()


def build(mesh, dims):
    NZ, NY, NX, NH = dims

    def body(states, head_weight, pair_order, row_example):
        mb, rows, width = states.shape
        vocab = head_weight.shape[1]
        count = NZ * NY
        side = rows // 2
        rg, cg = side // NZ, vocab // NY
        quarter = rows // NX
        vm = pltpu.VMEM
        dma = pltpu.SemaphoreType.DMA
        hbm = pl.BlockSpec(memory_space=pl.ANY)
        return pl.pallas_call(
            functools.partial(kernel, dims),
            out_shape=(
                jax.ShapeDtypeStruct(states.shape, BF16),
                jax.ShapeDtypeStruct(head_weight.shape, BF16),
            ),
            in_specs=[pl.BlockSpec(memory_space=pltpu.SMEM), hbm, hbm, hbm],
            out_specs=(hbm, hbm),
            scratch_shapes=[
                vm((width, vocab), BF16),
                vm((vocab, width), BF16),
                vm((mb, rows, width), BF16),
                vm(row_example.shape, jnp.int32),
                vm((mb, rows, rows), BF16),
                vm((mb, rows, width), BF16),
                vm((mb, width, rows), BF16),
                vm((mb, 2, side // 2, vocab), F32),
                vm((mb, 2, side // 2, vocab), F32),
                vm((mb, 2, side // 2, vocab), F32),
                vm((mb, count, rg, cg), BF16),
                vm((count, rg, cg), BF16),
                vm((count, rg, cg), BF16),
                vm((mb, count, rg, cg), BF16),
                vm((mb, 2, count, rg, cg), BF16),
                vm((mb, rows, width), F32),
                vm((mb, NX, quarter, width), BF16),
                vm((mb, NX, quarter, width), BF16),
                vm((mb, quarter, width), BF16),
                vm((mb, quarter, width), BF16),
                vm((mb, NX, quarter, width), BF16),
                vm((mb, rows, width), BF16),
                vm((width, vocab), BF16),
                pltpu.SMEM((mb, count), jnp.int32),
                dma((3,)),
                dma((2,)),
                dma((mb, 2)),
                dma((mb, 2)),
            ]
            + [dma((mb,))] * 12,
            compiler_params=pltpu.CompilerParams(
                collective_id=0, has_side_effects=True, vmem_limit_bytes=56 * 1024 * 1024
            ),
        )(pair_order, states, head_weight, row_example)

    return jax.shard_map(
        body,
        mesh=mesh,
        in_specs=(P(None, None, "rep"), P("rep", "voc"), P(), P()),
        out_specs=(P(None, None, "rep"), P("rep", "voc")),
        check_vma=False,
    )


def solution(mesh):
    return build(mesh, (8, 4, 4, 2))
```

time: 189 us -> 106 us (0.56)
  the two profiles are of different devices: /device:TPU:80 before, /device:TPU:40 now
where the time goes in v1:
time: 106 us
  Pallas kernels  101 us (95%)
  local copies, waits for them, and re-layouts  4.51 us (4%)
    pallas_call x1, Pallas kernels, body(): pl.pallas_call(functools.partial(kernel, dims), out_shape=(jax.ShapeDtype...  101 us
    unnamed x2, local copies, waits for them, and re-layouts  4.51 us

profile of v1, /device:TPU:40, one launch (start us, length us, event | category | flops | bytes accessed | tf_op | source)
XLA Modules:
  0.0 105.8 jit_solution(10460545650966973358)
XLA Ops:
  0.6 100.6 %shard_map.59 = (bf16[2,256,384]{2,1,0:T(8,128)(2,1)}, bf16[384,2048]{1,0:T(8,128)(2,1)}) custom-call(s32[2,32]{1,0:T(2,128)} %pair_order.1, bf16[2,256,384]{2,1,0:T(8,128)(2,1)} %states_hbm.1, bf16[384,2048]{1,0:T(8,128)(2,1)} %weight_hbm.1, s32[2,32,256]{2,1,0:T(8,128)} %example_hbm.1), custom_call_target="tpu_custom_call" | custom-call | tf_op jit(solution)/shard_map/pallas_call | solution.py:352
  101.3 1.8 %copy.8 = bf16[2,256,384]{2,1,0:T(8,128)(2,1)} copy(bf16[2,256,384]{2,1,0:T(8,128)(2,1)} %get-tuple-element.4) | data formatting | bytes 786432
  103.0 2.7 %copy.9 = bf16[384,2048]{1,0:T(8,128)(2,1)} copy(bf16[384,2048]{1,0:T(8,128)(2,1)} %get-tuple-element.5) | data formatting | bytes 3145728

commit v2 on v0

v2 whole, which is shorter than its diff:
```python
import functools

import jax
import jax.numpy as jnp
from jax import lax
from jax.experimental import pallas as pl
from jax.experimental.pallas import tpu as pltpu
from jax.sharding import PartitionSpec as P

MESH = pl.DeviceIdType.MESH
SCALE = 0.0625
CUTS = 2
TALL = 16
F32, BF16 = jnp.float32, jnp.bfloat16
scope = jax.named_scope


def kernel(
    dims,
    order_hbm,
    states_hbm,
    weight_hbm,
    example_hbm,
    state_hbm,
    head_hbm,
    pair_order,
    weight,
    weight_t,
    states,
    examples,
    onehot,
    ordered,
    ordered_t,
    mine,
    sent,
    got,
    logits,
    pools,
    spread,
    grad,
    part,
    part_b,
    xin,
    half,
    half_in,
    total,
    state_out,
    head_out,
    partner,
    in_sem,
    out_sem,
    pair_send,
    pair_recv,
    one_send,
    one_recv,
    two_send,
    two_recv,
    fwd_send,
    fwd_recv,
    xs_send,
    xs_recv,
    y_send,
    y_recv,
    xg_send,
    xg_recv,
):
    NZ, NY, NX, NH = dims
    mb, rows, width = states.shape
    vocab = weight.shape[1]
    count = NZ * NY
    chunks = CUTS * mb
    crows = rows // CUTS
    srows = crows // 2
    rows_n = srows // TALL
    cols_n = count // rows_n
    cg = vocab // cols_n
    quarter = crows // NX

    rep, voc = lax.axis_index("rep"), lax.axis_index("voc")
    core = lax.rem(rep, 2)
    rid = rep // 2
    z, y = rid // NY, lax.rem(rid, NY)
    h, x = voc // NX, lax.rem(voc, NX)
    pair = {"rep": rid * 2 + 1 - core}
    across = {"voc": (NH - 1 - h) * NX + x}

    loads = [
        pltpu.make_async_copy(example_hbm, examples, in_sem.at[0]),
        pltpu.make_async_copy(states_hbm, states, in_sem.at[1]),
        pltpu.make_async_copy(weight_hbm, weight, in_sem.at[2]),
        pltpu.make_async_copy(order_hbm, pair_order, in_sem.at[3]),
    ]
    barrier = pltpu.get_barrier_semaphore()

    def greet():
        for k in range(1, count):
            pl.semaphore_signal(
                barrier,
                inc=1,
                device_id={"rep": lax.rem(rid + k, count) * 2 + core},
                device_id_type=MESH,
            )

        pl.semaphore_signal(barrier, inc=1, device_id=pair, device_id_type=MESH)
        for k in range(1, NX):
            pl.semaphore_signal(
                barrier, inc=1, device_id={"voc": h * NX + lax.rem(x + k, NX)}, device_id_type=MESH
            )
        pl.semaphore_signal(barrier, inc=1, device_id=across, device_id_type=MESH)

    def order():
        ids = lax.broadcasted_iota(jnp.int32, (rows, rows), 0)
        for m in range(mb):
            row = examples[m, pl.ds(rid, 1), :]
            onehot[m] = (ids == row).astype(BF16)
            ordered[m] = jnp.dot(onehot[m], states[m], preferred_element_type=F32).astype(BF16)

    def partials(side, target):
        left = []
        for q in range(chunks):
            at = pl.multiple_of((q % CUTS) * crows + side * srows, srows)
            left.append(ordered[q // CUTS, pl.ds(at, srows), :])
        left = jnp.concatenate(left, axis=0)

        @pl.loop(0, 4)
        def _(j):
            cols = pl.ds(pl.multiple_of(j * (vocab // 4), vocab // 4), vocab // 4)
            out = jnp.dot(left, weight[:, cols], preferred_element_type=F32)
            for q in range(chunks):
                target[q, :, cols] = out[q * srows : (q + 1) * srows]

    def pair_copy(q):
        return pltpu.make_async_remote_copy(
            src_ref=sent.at[q],
            dst_ref=got.at[q],
            send_sem=pair_send.at[q],
            recv_sem=pair_recv.at[q],
            device_id=pair,
            device_id_type=MESH,
        )

    def send(r, src, dst, send_sem, recv_sem):
        pltpu.make_async_remote_copy(
            src_ref=src,
            dst_ref=dst,
            send_sem=send_sem,
            recv_sem=recv_sem,
            device_id={"rep": r * 2 + core},
            device_id_type=MESH,
        ).start()

    def settle(q):
        @pl.loop(0, 4)
        def _(j):
            cols = pl.ds(pl.multiple_of(j * (vocab // 4), vocab // 4), vocab // 4)
            both = (mine[q, :, cols] + got[q, :, cols]).astype(BF16)
            for i in range(cols_n // 4):
                piece = both[:, i * cg : (i + 1) * cg].reshape(rows_n, TALL, cg)
                logits[q, pl.ds((j * (cols_n // 4) + i) * rows_n, rows_n)] = piece

        @pl.loop(1, count)
        def _(k):
            r = lax.rem(rid + k, count)
            send(r, logits.at[q, r], pools[q].at[rid], one_send.at[q], one_recv.at[q])

        pltpu.make_async_copy(logits.at[q, rid], pools[q].at[rid], one_recv.at[q]).start()

    def tables():
        loads[3].wait()
        for m in range(mb):

            @pl.loop(0, count)
            def _(r):
                found = jnp.int32(0)
                for k in range(count):
                    found += jnp.where(pair_order[m, k] == r, pair_order[m, (k + 1) % count], 0)
                partner[m, r] = found

    def turn():
        for m in range(mb):
            ordered_t[:, m * rows : (m + 1) * rows] = ordered[m].T

        @pl.loop(0, 4)
        def _(j):
            at = pl.multiple_of(j * (vocab // 4), vocab // 4)
            weight_t[pl.ds(at, vocab // 4), :] = weight[:, pl.ds(at, vocab // 4)].T

    def compare(q):
        pool, batch = pools[q], 8

        def differ(r):
            own, other = pool[r], pool[partner[q // CUTS, r]]
            spread[q, r] = (SCALE * (own.astype(F32) - other.astype(F32))).astype(BF16)

        @pl.loop(0, count // batch)
        def _(b):
            for i in range(batch):
                differ(lax.rem(rid + 1 + b * batch + i, count))
            for i in range(batch - 1):
                r = lax.rem(rid + 1 + b * batch + i, count)
                send(r, spread.at[q, r], grad.at[q, core, rid], two_send.at[q], two_recv.at[q])

            @pl.when(b < count // batch - 1)
            def _():
                r = lax.rem(rid + 1 + b * batch + batch - 1, count)
                send(r, spread.at[q, r], grad.at[q, core, rid], two_send.at[q], two_recv.at[q])

        pltpu.make_async_copy(spread.at[q, rid], grad.at[q, core, rid], two_recv.at[q]).start()

    def await_ref(ref, sem):
        pltpu.make_async_copy(ref, ref, sem).wait()

    def forward(q):
        return pltpu.make_async_remote_copy(
            src_ref=grad.at[q, core],
            dst_ref=grad.at[q, core],
            send_sem=fwd_send.at[q],
            recv_sem=fwd_recv.at[q],
            device_id=pair,
            device_id_type=MESH,
        )

    def scatter(q, k):
        xt = lax.rem(x + k, NX)
        return pltpu.make_async_remote_copy(
            src_ref=part_b.at[q, xt],
            dst_ref=xin.at[q, x],
            send_sem=xs_send.at[q],
            recv_sem=xs_recv.at[q],
            device_id={"voc": h * NX + xt},
            device_id_type=MESH,
        )

    def gather(q, k):
        xt = lax.rem(x + k, NX)
        return pltpu.make_async_remote_copy(
            src_ref=total.at[q, x],
            dst_ref=total.at[q, x],
            send_sem=xg_send.at[q],
            recv_sem=xg_recv.at[q],
            device_id={"voc": h * NX + xt},
            device_id_type=MESH,
        )

    def cross(q):
        return pltpu.make_async_remote_copy(
            src_ref=half.at[q],
            dst_ref=half_in.at[q],
            send_sem=y_send.at[q],
            recv_sem=y_recv.at[q],
            device_id=across,
            device_id_type=MESH,
        )

    def others(ref, sem):
        few = ref.at[pl.ds(0, NX - 1)]
        pltpu.make_async_copy(few, few, sem).wait()

    def block(q, j):
        return grad[q, :, pl.ds(j * rows_n, rows_n)].reshape(crows, cg)

    def state_part(q):
        lhs = jnp.concatenate([block(q, j) for j in range(cols_n)], axis=1)
        out = jnp.dot(lhs, weight_t[...], preferred_element_type=F32)
        part[q] = out
        part_b[q] = out.astype(BF16).reshape(NX, quarter, width)

    def head():
        per = cols_n // 8
        wide = vocab // 8
        for j in range(8):
            cols = pl.ds(j * wide, wide)
            right = jnp.concatenate(
                [
                    jnp.concatenate([block(q, j * per + i) for i in range(per)], axis=1)
                    for q in range(chunks)
                ],
                axis=0,
            )
            out = jnp.dot(ordered_t[...], right, preferred_element_type=F32)
            head_out[:, cols] = out.astype(BF16)
            pltpu.make_async_copy(head_out.at[:, cols], head_hbm.at[:, cols], out_sem.at[0]).start()

    def sum_x(q):
        acc = part[q, pl.ds(pl.multiple_of(x * quarter, quarter), quarter), :]
        for k in range(1, NX):
            acc += xin[q, lax.rem(x + k, NX)].astype(F32)
        half[q] = acc.astype(BF16)

    def sum_h(q):
        total[q, x] = (half[q].astype(F32) + half_in[q].astype(F32)).astype(BF16)

    def restore(m):
        state_out[m] = lax.dot_general(
            onehot[m],
            total[CUTS * m : CUTS * m + CUTS].reshape(rows, width),
            (((0,), (0,)), ((), ())),
            preferred_element_type=F32,
        ).astype(BF16)
        pltpu.make_async_copy(state_out.at[m], state_hbm.at[m], out_sem.at[1]).start()

    def x_stage(q):
        with scope(f"xs_wait{q}"):
            others(xin.at[q], xs_recv.at[q])
        sum_x(q)
        cross(q).start()

    def y_stage(q):
        with scope(f"y_wait{q}"):
            cross(q).wait_recv()
        sum_h(q)
        for k in range(1, NX):
            gather(q, k).start()

    def done(q):
        with scope(f"xg_wait{q}"):
            others(total.at[q], xg_recv.at[q])

    for load in loads:
        load.start()
    with scope("greet"):
        greet()
    with scope("load"):
        loads[0].wait()
        loads[1].wait()
    with scope("order"):
        order()
    with scope("loadw"):
        loads[2].wait()
    with scope("partial0"):
        partials(1 - core, sent)
    with scope("barrier"):
        pl.semaphore_wait(barrier, count - 1 + 1 + NX - 1 + 1)
    for q in range(chunks):
        pair_copy(q).start()
    with scope("partial1"):
        partials(core, mine)
    for q in range(chunks):
        with scope(f"pairwait{q}"):
            pair_copy(q).wait_recv()
        with scope(f"settle{q}"):
            settle(q)
    with scope("tables"):
        tables()
    with scope("turn"):
        turn()
    for q in range(chunks):
        with scope(f"wait1_{q}"):
            await_ref(pools[q], one_recv.at[q])
        with scope(f"compare{q}"):
            compare(q)
    for q in range(chunks + 3):
        last = q == chunks - 1
        if q < chunks:
            with scope(f"wait2_{q}"):
                await_ref(grad.at[q, core], two_recv.at[q])
            with scope(f"forward{q}"):
                forward(q).start()
                forward(q).wait_recv()
            with scope(f"state_part{q}"):
                state_part(q)
            for k in range(1, NX):
                scatter(q, k).start()
            if last:
                x_stage(q - 1)
                y_stage(q - 2)
                with scope("head"):
                    head()
        if q == chunks:
            x_stage(q - 1)
            y_stage(q - 2)
        elif not last:
            if 0 <= q - 1 < chunks:
                x_stage(q - 1)
            if 0 <= q - 2 < chunks:
                y_stage(q - 2)
        if 0 <= q - 3 < chunks:
            done(q - 3)
            if q - 3 < chunks - 1 and (q - 3) % CUTS == CUTS - 1:
                with scope(f"restore{q-3}"):
                    restore((q - 3) // CUTS)
    with scope("restore"):
        restore(mb - 1)

    with scope("drain"):
        most = logits.at[0, pl.ds(0, count - 1)]
        for q in range(chunks):
            pair_copy(q).wait_send()
            await_ref(most, one_send.at[q])
            await_ref(most, two_send.at[q])
            forward(q).wait_send()
            others(part_b.at[q], xs_send.at[q])
            others(total.at[q], xg_send.at[q])
            cross(q).wait_send()
        pltpu.make_async_copy(head_out, head_hbm, out_sem.at[0]).wait()
        pltpu.make_async_copy(state_out, state_hbm, out_sem.at[1]).wait()


def finish(state_in, head_in, state_out, head_out, state, head, in_sem, out_sem):
    pieces = 4
    step = head.shape[0] // pieces
    moves = []
    for p in range(pieces):
        at = pl.ds(p * step, step)
        moves.append((head_in.at[at], head.at[at], head_out.at[at]))
    for m in range(state.shape[0]):
        moves.append((state_in.at[m], state.at[m], state_out.at[m]))
    ins = [pltpu.make_async_copy(a, b, in_sem.at[i]) for i, (a, b, _) in enumerate(moves)]
    outs = [pltpu.make_async_copy(b, c, out_sem.at[i]) for i, (_, b, c) in enumerate(moves)]
    for copy in ins:
        copy.start()
    for copy_in, copy_out in zip(ins, outs):
        copy_in.wait()
        copy_out.start()
    for copy in outs:
        copy.wait()


def build(mesh, dims):
    NZ, NY, NX, NH = dims

    def body(states, head_weight, pair_order, row_example):
        mb, rows, width = states.shape
        vocab = head_weight.shape[1]
        count = NZ * NY
        chunks = CUTS * mb
        crows = rows // CUTS
        srows = crows // 2
        slot = (count, TALL, vocab * srows // (count * TALL))
        quarter = crows // NX
        vm = pltpu.VMEM
        dma = pltpu.SemaphoreType.DMA
        hbm = pl.BlockSpec(memory_space=pl.ANY)
        shapes = (
            jax.ShapeDtypeStruct(states.shape, BF16),
            jax.ShapeDtypeStruct(head_weight.shape, BF16),
        )
        made = pl.pallas_call(
            functools.partial(kernel, dims),
            out_shape=shapes,
            in_specs=[hbm, hbm, hbm, hbm],
            out_specs=(hbm, hbm),
            scratch_shapes=[
                pltpu.SMEM((mb, count), jnp.int32),
                vm((width, vocab), BF16),
                vm((vocab, width), BF16),
                vm((mb, rows, width), BF16),
                vm(row_example.shape, jnp.int32),
                vm((mb, rows, rows), BF16),
                vm((mb, rows, width), BF16),
                vm((width, mb * rows), BF16),
                vm((chunks, srows, vocab), F32),
                vm((chunks, srows, vocab), F32),
                vm((chunks, srows, vocab), F32),
                vm((chunks, *slot), BF16),
            ]
            + [[vm(slot, BF16)] * chunks]
            + [
                vm((chunks, *slot), BF16),
                vm((chunks, 2, *slot), BF16),
                vm((chunks, crows, width), F32),
                vm((chunks, NX, quarter, width), BF16),
                vm((chunks, NX, quarter, width), BF16),
                vm((chunks, quarter, width), BF16),
                vm((chunks, quarter, width), BF16),
                vm((chunks, NX, quarter, width), BF16),
                vm((mb, rows, width), BF16),
                vm((width, vocab), BF16),
                pltpu.SMEM((mb, count), jnp.int32),
                dma((4,)),
                dma((2,)),
            ]
            + [dma((chunks,))] * 14,
            compiler_params=pltpu.CompilerParams(
                collective_id=0, has_side_effects=True, vmem_limit_bytes=60 * 1024 * 1024
            ),
        )(pair_order, states, head_weight, row_example)
        pieces = 4 + mb
        return pl.pallas_call(
            finish,
            out_shape=shapes,
            in_specs=[hbm, hbm],
            out_specs=(hbm, hbm),
            scratch_shapes=[
                vm(states.shape, BF16),
                vm(head_weight.shape, BF16),
                dma((pieces,)),
                dma((pieces,)),
            ],
            compiler_params=pltpu.CompilerParams(vmem_limit_bytes=60 * 1024 * 1024),
        )(*made)

    return jax.shard_map(
        body,
        mesh=mesh,
        in_specs=(P(None, None, "rep"), P("rep", "voc"), P(), P()),
        out_specs=(P(None, None, "rep"), P("rep", "voc")),
        check_vma=False,
    )


def solution(mesh):
    return build(mesh, (8, 4, 4, 2))
```

time: 189 us -> 87.8 us (0.46)
  the two profiles are of different devices: /device:TPU:80 before, /device:TPU:1 now
where the time goes in v2:
time: 87.8 us; the launch traced here: 87.6 us
  Pallas kernels  86.9 us (99%)
    pallas_call x1, Pallas kernels, body(): pl.pallas_call(functools.partial(kernel, dims), out_shape=shapes, in_spec...  84.6 us
    pallas_call x1, Pallas kernels, body(): pl.pallas_call(finish, out_shape=shapes, in_specs=[hbm, hbm], out_specs=(...  2.36 us

profile of v2, /device:TPU:1, one launch (start us, length us, event | category | flops | bytes accessed | tf_op | source)
XLA Modules:
  0.0 87.6 jit_solution(2335742713592237858)
XLA Ops:
  0.6 84.6 %shard_map.59 = (bf16[2,256,384]{2,1,0:T(8,128)(2,1)}, bf16[384,2048]{1,0:T(8,128)(2,1)}) custom-call(s32[2,32]{1,0:T(2,128)} %order_hbm.1, bf16[2,256,384]{2,1,0:T(8,128)(2,1)} %states_hbm.1, bf16[384,2048]{1,0:T(8,128)(2,1)} %weight_hbm.1, s32[2,32,256]{2,1,0:T(8,128)} %example_hbm.1), custom_call_target="tpu_custom_call" | custom-call | tf_op jit(solution)/shard_map/pallas_call | solution.py:438
  85.2 2.4 %shard_map.60 = (bf16[2,256,384]{2,1,0:T(8,128)(2,1)}, bf16[384,2048]{1,0:T(8,128)(2,1)}) custom-call(bf16[2,256,384]{2,1,0:T(8,128)(2,1)} %get-tuple-element.4.state_in, bf16[384,2048]{1,0:T(8,128)(2,1)} %get-tuple-element.5.head_in), custom_call_target="tpu_custom_call" | custom-call | tf_op jit(solution)/shard_map/pallas_call | solution.py:479

commit v3 on v2

v3 whole, which is shorter than its diff:
```python
import functools

import jax
import jax.numpy as jnp
from jax import lax
from jax.experimental import pallas as pl
from jax.experimental.pallas import tpu as pltpu
from jax.sharding import PartitionSpec as P

MESH = pl.DeviceIdType.MESH
SCALE = 0.0625
PLAN = ((0, 64), (0, 64), (1, 64), (1, 64))
TALL = 16
F32, BF16 = jnp.float32, jnp.bfloat16
scope = jax.named_scope


def kernel(
    dims,
    order_hbm,
    states_hbm,
    weight_hbm,
    example_hbm,
    state_hbm,
    head_hbm,
    pair_order,
    weight,
    weight_t,
    states,
    examples,
    onehot,
    ordered,
    ordered_t,
    mine,
    sent,
    got,
    logits,
    pools,
    spread,
    grad,
    part,
    part_b,
    xin,
    half,
    half_in,
    final,
    total,
    state_out,
    head_out,
    partner,
    in_sem,
    out_sem,
    pair_send,
    pair_recv,
    one_send,
    one_recv,
    two_send,
    two_recv,
    fwd_send,
    fwd_recv,
    turn_sem,
    xs_send,
    xs_recv,
    y_send,
    y_recv,
    xg_send,
    xg_recv,
):
    NZ, NY, NX, NH = dims
    mb, rows, width = states.shape
    vocab = weight.shape[1]
    count = NZ * NY
    chunks = len(PLAN)
    micro = [m for m, _ in PLAN]
    srows = [n for _, n in PLAN]
    first = [2 * sum(n for p, n in PLAN[:q] if p == micro[q]) for q in range(chunks)]
    base = [sum(srows[:q]) for q in range(chunks)]
    rows_n = [n // TALL for n in srows]
    cols_n = [count // n for n in rows_n]
    cgs = [vocab // n for n in cols_n]
    quarter = [n // NX for n in srows]

    rep, voc = lax.axis_index("rep"), lax.axis_index("voc")
    core = lax.rem(rep, 2)
    rid = rep // 2
    z, y = rid // NY, lax.rem(rid, NY)
    h, x = voc // NX, lax.rem(voc, NX)
    pair = {"rep": rid * 2 + 1 - core}
    across = {"voc": (NH - 1 - h) * NX + x}

    def along(k, other):
        there = 1 - core if other else core
        return {"rep": rid * 2 + there, "voc": h * NX + lax.rem(x + k, NX)}


    loads = [
        pltpu.make_async_copy(example_hbm, examples, in_sem.at[0]),
        pltpu.make_async_copy(states_hbm, states, in_sem.at[1]),
        pltpu.make_async_copy(weight_hbm, weight, in_sem.at[2]),
        pltpu.make_async_copy(order_hbm, pair_order, in_sem.at[3]),
    ]
    barrier = pltpu.get_barrier_semaphore()

    def greet():
        for k in sorted(range(1, count), key=lambda k: -min(k, count - k)):
            pl.semaphore_signal(
                barrier,
                inc=1,
                device_id={"rep": lax.rem(rid + k, count) * 2 + core},
                device_id_type=MESH,
            )

        pl.semaphore_signal(barrier, inc=1, device_id=pair, device_id_type=MESH)
        for k in range(1, NX):
            for other in range(2):
                pl.semaphore_signal(
                    barrier, inc=1, device_id=along(k, other), device_id_type=MESH
                )
        pl.semaphore_signal(barrier, inc=1, device_id=across, device_id_type=MESH)

    def order():
        ids = lax.broadcasted_iota(jnp.int32, (rows, rows), 0)
        for m in range(mb):
            row = examples[m, pl.ds(rid, 1), :]
            onehot[m] = (ids == row).astype(BF16)
            ordered[m] = jnp.dot(onehot[m], states[m], preferred_element_type=F32).astype(BF16)

    def partials(side, target):
        left = []
        for q in range(chunks):
            at = pl.multiple_of(first[q] + side * srows[q], srows[q])
            left.append(ordered[micro[q], pl.ds(at, srows[q]), :])
        left = jnp.concatenate(left, axis=0)

        @pl.loop(0, 4)
        def _(j):
            cols = pl.ds(pl.multiple_of(j * (vocab // 4), vocab // 4), vocab // 4)
            out = jnp.dot(left, weight[:, cols], preferred_element_type=F32)
            target[:, cols] = out

    def pair_copy(q):
        return pltpu.make_async_remote_copy(
            src_ref=sent.at[pl.ds(base[q], srows[q])],
            dst_ref=got.at[pl.ds(base[q], srows[q])],
            send_sem=pair_send.at[q],
            recv_sem=pair_recv.at[q],
            device_id=pair,
            device_id_type=MESH,
        )

    def send(r, src, dst, send_sem, recv_sem):
        pltpu.make_async_remote_copy(
            src_ref=src,
            dst_ref=dst,
            send_sem=send_sem,
            recv_sem=recv_sem,
            device_id={"rep": r * 2 + core},
            device_id_type=MESH,
        ).start()

    def settle(q):
        rn, cg, per = rows_n[q], cgs[q], cols_n[q] // 4
        at = pl.ds(base[q], srows[q])

        @pl.loop(0, 4)
        def _(j):
            cols = pl.ds(pl.multiple_of(j * (vocab // 4), vocab // 4), vocab // 4)
            both = (mine[at, cols] + got[at, cols]).astype(BF16)
            for i in range(per):
                piece = both[:, i * cg : (i + 1) * cg].reshape(rn, TALL, cg)
                logits[q][pl.ds((j * per + i) * rn, rn)] = piece

        @pl.loop(1, count)
        def _(k):
            r = lax.rem(rid + k, count)
            send(r, logits[q].at[r], pools[q].at[rid], one_send.at[q], one_recv.at[q])

        pltpu.make_async_copy(logits[q].at[rid], pools[q].at[rid], one_recv.at[q]).start()

    def tables():
        loads[3].wait()
        for m in range(mb):

            @pl.loop(0, count)
            def _(r):
                found = jnp.int32(0)
                for k in range(count):
                    found += jnp.where(pair_order[m, k] == r, pair_order[m, (k + 1) % count], 0)
                partner[m, r] = found

    def turn():
        for m in range(mb):
            ordered_t[:, m * rows : (m + 1) * rows] = ordered[m].T

        @pl.loop(0, 4)
        def _(j):
            at = pl.multiple_of(j * (vocab // 4), vocab // 4)
            weight_t[core, pl.ds(at, vocab // 4), :] = weight[:, pl.ds(at, vocab // 4)].T

    def compare(q):
        pool, batch = pools[q], 8

        def differ(r):
            own, other = pool[r], pool[partner[micro[q], r]]
            spread[q][r] = (SCALE * (own.astype(F32) - other.astype(F32))).astype(BF16)

        @pl.loop(0, count // batch)
        def _(b):
            for i in range(batch):
                differ(lax.rem(rid + 1 + b * batch + i, count))
            for i in range(batch - 1):
                r = lax.rem(rid + 1 + b * batch + i, count)
                send(r, spread[q].at[r], grad[q].at[core, rid], two_send.at[q], two_recv.at[q])

            @pl.when(b < count // batch - 1)
            def _():
                r = lax.rem(rid + 1 + b * batch + batch - 1, count)
                send(r, spread[q].at[r], grad[q].at[core, rid], two_send.at[q], two_recv.at[q])

        pltpu.make_async_copy(spread[q].at[rid], grad[q].at[core, rid], two_recv.at[q]).start()

    def await_ref(ref, sem):
        pltpu.make_async_copy(ref, ref, sem).wait()

    def forward(q):
        return pltpu.make_async_remote_copy(
            src_ref=grad[q].at[core],
            dst_ref=grad[q].at[core],
            send_sem=fwd_send.at[q],
            recv_sem=fwd_recv.at[q],
            device_id=pair,
            device_id_type=MESH,
        )

    def turned():
        return pltpu.make_async_remote_copy(
            src_ref=weight_t.at[core],
            dst_ref=weight_t.at[core],
            send_sem=turn_sem.at[0],
            recv_sem=turn_sem.at[1],
            device_id=pair,
            device_id_type=MESH,
        )

    def scatter(q, k):
        return pltpu.make_async_remote_copy(
            src_ref=part_b[q].at[lax.rem(x + k, NX)],
            dst_ref=xin[q].at[x],
            send_sem=xs_send.at[q],
            recv_sem=xs_recv.at[q],
            device_id=along(k, 0),
            device_id_type=MESH,
        )

    def gather(q):
        dst = total[q].at[core * NX + x]
        for k in sorted(range(NX), key=lambda k: -min(k, NX - k)):
            for other in range(2):
                if k or other:
                    pltpu.make_async_remote_copy(
                        src_ref=final[q].at[1 - core if other else core],
                        dst_ref=dst,
                        send_sem=xg_send.at[q],
                        recv_sem=xg_recv.at[q],
                        device_id=along(k, other),
                        device_id_type=MESH,
                    ).start()
        total[q][core * NX + x] = final[q][core]

    def cross(q):
        return pltpu.make_async_remote_copy(
            src_ref=half[q],
            dst_ref=half_in[q],
            send_sem=y_send.at[q],
            recv_sem=y_recv.at[q],
            device_id=across,
            device_id_type=MESH,
        )

    def others(ref, sem):
        few = ref.at[pl.ds(0, ref.shape[0] - 1)]
        pltpu.make_async_copy(few, few, sem).wait()

    def state_part(q):
        lhs = jnp.concatenate(
            [
                grad[q][core, pl.ds(j * rows_n[q], rows_n[q])].reshape(srows[q], cgs[q])
                for j in range(cols_n[q])
            ],
            axis=1,
        )
        for w in range(2):
            out = jnp.dot(lhs, weight_t[w], preferred_element_type=F32)
            part[q][w] = out
            part_b[q][:, w] = out.reshape(NX, quarter[q], width).astype(BF16)

    def head():
        wide = vocab // 8
        for j in range(8):
            cols = pl.ds(j * wide, wide)
            right = []
            for q in range(chunks):
                per, rn = cols_n[q] // 8, rows_n[q]
                right.append(
                    jnp.concatenate(
                        [
                            grad[q][:, pl.ds((j * per + i) * rn, rn)].reshape(2 * srows[q], cgs[q])
                            for i in range(per)
                        ],
                        axis=1,
                    )
                )
            right = jnp.concatenate(right, axis=0)
            out = jnp.dot(ordered_t[...], right, preferred_element_type=F32)
            head_out[:, cols] = out.astype(BF16)
            pltpu.make_async_copy(head_out.at[:, cols], head_hbm.at[:, cols], out_sem.at[0]).start()

    def sum_x(q):
        acc = part[q][:, pl.ds(pl.multiple_of(x * quarter[q], quarter[q]), quarter[q]), :]
        for k in range(1, NX):
            acc += xin[q][lax.rem(x + k, NX)].astype(F32)
        half[q][...] = acc.astype(BF16)

    def sum_h(q):
        final[q][...] = (half[q][...].astype(F32) + half_in[q][...].astype(F32)).astype(BF16)

    def restore(m):
        rows_of = [
            total[q][...].astype(F32).reshape(2 * srows[q], width).astype(BF16)
            for q in range(chunks)
            if micro[q] == m
        ]
        state_out[m] = lax.dot_general(
            onehot[m],
            jnp.concatenate(rows_of, axis=0),
            (((0,), (0,)), ((), ())),
            preferred_element_type=F32,
        ).astype(BF16)
        pltpu.make_async_copy(state_out.at[m], state_hbm.at[m], out_sem.at[1]).start()

    def x_stage(q):
        with scope(f"xs_wait{q}"):
            others(xin[q], xs_recv.at[q])
        sum_x(q)
        cross(q).start()

    def y_stage(q):
        with scope(f"y_wait{q}"):
            cross(q).wait_recv()
        sum_h(q)
        gather(q)

    def done(q):
        with scope(f"xg_wait{q}"):
            others(total[q], xg_recv.at[q])

    for load in loads:
        load.start()
    with scope("greet"):
        greet()
    with scope("load"):
        loads[0].wait()
        loads[1].wait()
    with scope("order"):
        order()
    with scope("loadw"):
        loads[2].wait()
    with scope("partial0"):
        partials(1 - core, sent)
    with scope("partial1"):
        partials(core, mine)
    with scope("barrier"):
        pl.semaphore_wait(barrier, count - 1 + 1 + 2 * (NX - 1) + 1)
    for q in range(chunks):
        pair_copy(q).start()
    for q in range(chunks):
        with scope(f"pairwait{q}"):
            pair_copy(q).wait_recv()
        with scope(f"settle{q}"):
            settle(q)
    with scope("turn"):
        turn()
    turned().start()
    with scope("tables"):
        tables()
    for q in range(chunks):
        with scope(f"wait1_{q}"):
            await_ref(pools[q], one_recv.at[q])
        with scope(f"compare{q}"):
            compare(q)
    turned().wait_recv()
    for q in range(chunks):
        with scope(f"wait2_{q}"):
            await_ref(grad[q].at[core], two_recv.at[q])
        forward(q).start()
        with scope(f"state_part{q}"):
            state_part(q)
        for k in sorted(range(1, NX), key=lambda k: -min(k, NX - k)):
            scatter(q, k).start()
        if q > 0:
            x_stage(q - 1)
        if q > 2:
            y_stage(q - 3)
    x_stage(chunks - 1)
    y_stage(chunks - 3)
    with scope("fwd_wait"):
        for q in range(chunks):
            forward(q).wait_recv()
    with scope("head"):
        head()
    y_stage(chunks - 2)
    y_stage(chunks - 1)
    for m in range(mb):
        for q in range(chunks):
            if micro[q] == m:
                done(q)
        with scope(f"restore{m}"):
            restore(m)

    with scope("drain"):
        turned().wait_send()
        for q in range(chunks):
            pair_copy(q).wait_send()
            others(logits[q], one_send.at[q])
            others(spread[q], two_send.at[q])
            forward(q).wait_send()
            others(part_b[q], xs_send.at[q])
            others(total[q], xg_send.at[q])
            cross(q).wait_send()
        pltpu.make_async_copy(head_out, head_hbm, out_sem.at[0]).wait()
        pltpu.make_async_copy(state_out, state_hbm, out_sem.at[1]).wait()


def finish(state_in, head_in, state_out, head_out, state, head, in_sem, out_sem):
    pieces = 4
    step = head.shape[0] // pieces
    moves = []
    for p in range(pieces):
        at = pl.ds(p * step, step)
        moves.append((head_in.at[at], head.at[at], head_out.at[at]))
    for m in range(state.shape[0]):
        moves.append((state_in.at[m], state.at[m], state_out.at[m]))
    ins = [pltpu.make_async_copy(a, b, in_sem.at[i]) for i, (a, b, _) in enumerate(moves)]
    outs = [pltpu.make_async_copy(b, c, out_sem.at[i]) for i, (_, b, c) in enumerate(moves)]
    for copy in ins:
        copy.start()
    for copy_in, copy_out in zip(ins, outs):
        copy_in.wait()
        copy_out.start()
    for copy in outs:
        copy.wait()


def build(mesh, dims):
    NZ, NY, NX, NH = dims

    def body(states, head_weight, pair_order, row_example):
        mb, rows, width = states.shape
        vocab = head_weight.shape[1]
        count = NZ * NY
        chunks = len(PLAN)
        srows = [n for _, n in PLAN]
        slots = [(count, TALL, vocab * n // (count * TALL)) for n in srows]
        quarter = [n // NX for n in srows]
        vm = pltpu.VMEM
        dma = pltpu.SemaphoreType.DMA
        hbm = pl.BlockSpec(memory_space=pl.ANY)
        shapes = (
            jax.ShapeDtypeStruct(states.shape, BF16),
            jax.ShapeDtypeStruct(head_weight.shape, BF16),
        )
        made = pl.pallas_call(
            functools.partial(kernel, dims),
            out_shape=shapes,
            in_specs=[hbm, hbm, hbm, hbm],
            out_specs=(hbm, hbm),
            scratch_shapes=[
                pltpu.SMEM((mb, count), jnp.int32),
                vm((width, vocab), BF16),
                vm((2, vocab, width), BF16),
                vm((mb, rows, width), BF16),
                vm(row_example.shape, jnp.int32),
                vm((mb, rows, rows), BF16),
                vm((mb, rows, width), BF16),
                vm((width, mb * rows), BF16),
                vm((sum(srows), vocab), F32),
                vm((sum(srows), vocab), F32),
                vm((sum(srows), vocab), F32),
                [vm(slot, BF16) for slot in slots],
                [vm(slot, BF16) for slot in slots],
                [vm(slot, BF16) for slot in slots],
                [vm((2, *slot), BF16) for slot in slots],
                [vm((2, n, width), F32) for n in srows],
                [vm((NX, 2, n, width), BF16) for n in quarter],
                [vm((NX, 2, n, width), BF16) for n in quarter],
                [vm((2, n, width), BF16) for n in quarter],
                [vm((2, n, width), BF16) for n in quarter],
                [vm((2, n, width), BF16) for n in quarter],
                [vm((2 * NX, n, width), BF16) for n in quarter],
                vm((mb, rows, width), BF16),
                vm((width, vocab), BF16),
                pltpu.SMEM((mb, count), jnp.int32),
                dma((4,)),
                dma((2,)),
            ]
            + [dma((chunks,))] * 8
            + [dma((2,))]
            + [dma((chunks,))] * 6,
            compiler_params=pltpu.CompilerParams(
                collective_id=0, has_side_effects=True, vmem_limit_bytes=60 * 1024 * 1024
            ),
        )(pair_order, states, head_weight, row_example)
        pieces = 4 + mb
        return pl.pallas_call(
            finish,
            out_shape=shapes,
            in_specs=[hbm, hbm],
            out_specs=(hbm, hbm),
            scratch_shapes=[
                vm(states.shape, BF16),
                vm(head_weight.shape, BF16),
                dma((pieces,)),
                dma((pieces,)),
            ],
            compiler_params=pltpu.CompilerParams(vmem_limit_bytes=60 * 1024 * 1024),
        )(*made)

    return jax.shard_map(
        body,
        mesh=mesh,
        in_specs=(P(None, None, "rep"), P("rep", "voc"), P(), P()),
        out_specs=(P(None, None, "rep"), P("rep", "voc")),
        check_vma=False,
    )


def solution(mesh):
    return build(mesh, (8, 4, 4, 2))
```

time: 87.8 us -> 84.5 us (0.962)
  Pallas kernels: 86.9 us -> 83.7 us
    pallas_call x1, Pallas kernels: 84.6 us -> 81.3 us  [body(): pl.pallas_call(functools.partial(kernel, dims), out_shape=shapes, in_spec...]
where the time goes in v3:
time: 84.5 us; the launch traced here: 84.3 us
  Pallas kernels  83.7 us (99%)
    pallas_call x1, Pallas kernels, body(): pl.pallas_call(functools.partial(kernel, dims), out_shape=shapes, in_spec...  81.3 us
    pallas_call x1, Pallas kernels, body(): pl.pallas_call(finish, out_shape=shapes, in_specs=[hbm, hbm], out_specs=(...  2.36 us

profile of v3, /device:TPU:1, one launch (start us, length us, event | category | flops | bytes accessed | tf_op | source)
XLA Modules:
  0.0 84.3 jit_solution(14761456515202581745)
XLA Ops:
  0.6 81.3 %shard_map.59 = (bf16[2,256,384]{2,1,0:T(8,128)(2,1)}, bf16[384,2048]{1,0:T(8,128)(2,1)}) custom-call(s32[2,32]{1,0:T(2,128)} %order_hbm.1, bf16[2,256,384]{2,1,0:T(8,128)(2,1)} %states_hbm.1, bf16[384,2048]{1,0:T(8,128)(2,1)} %weight_hbm.1, s32[2,32,256]{2,1,0:T(8,128)} %example_hbm.1), custom_call_target="tpu_custom_call" | custom-call | tf_op jit(solution)/shard_map/pallas_call | solution.py:472
  81.9 2.4 %shard_map.60 = (bf16[2,256,384]{2,1,0:T(8,128)(2,1)}, bf16[384,2048]{1,0:T(8,128)(2,1)}) custom-call(bf16[2,256,384]{2,1,0:T(8,128)(2,1)} %get-tuple-element.4.state_in, bf16[384,2048]{1,0:T(8,128)(2,1)} %get-tuple-element.5.head_in), custom_call_target="tpu_custom_call" | custom-call | tf_op jit(solution)/shard_map/pallas_call | solution.py:514

commit v4 on v3

--- a/solution.py
+++ b/solution.py
@@ -9,7 +9,8 @@
 
 MESH = pl.DeviceIdType.MESH
 SCALE = 0.0625
-PLAN = ((0, 64), (0, 64), (1, 64), (1, 64))
+GROUPS = ((0, (32, 32)), (0, (64,)), (1, (64,)), (1, (64,)))
+PLAN = [(g, sum(ns[:i]), n) for g, (_, ns) in enumerate(GROUPS) for i, n in enumerate(ns)]
 TALL = 16
 F32, BF16 = jnp.float32, jnp.bfloat16
 scope = jax.named_scope
@@ -71,14 +72,17 @@
     vocab = weight.shape[1]
     count = NZ * NY
     chunks = len(PLAN)
-    micro = [m for m, _ in PLAN]
-    srows = [n for _, n in PLAN]
-    first = [2 * sum(n for p, n in PLAN[:q] if p == micro[q]) for q in range(chunks)]
+    groups = len(GROUPS)
+    micro = [m for m, _ in GROUPS]
+    gs = [sum(ns) for _, ns in GROUPS]
+    first = [2 * sum(n for p, n in zip(micro[:g], gs) if p == micro[g]) for g in range(groups)]
+    of = [[q for q in range(chunks) if PLAN[q][0] == g] for g in range(groups)]
+    srows = [n for _, _, n in PLAN]
     base = [sum(srows[:q]) for q in range(chunks)]
     rows_n = [n // TALL for n in srows]
     cols_n = [count // n for n in rows_n]
     cgs = [vocab // n for n in cols_n]
-    quarter = [n // NX for n in srows]
+    quarter = [n // NX for n in gs]
 
     rep, voc = lax.axis_index("rep"), lax.axis_index("voc")
     core = lax.rem(rep, 2)
@@ -128,25 +132,33 @@
     def partials(side, target):
         left = []
         for q in range(chunks):
-            at = pl.multiple_of(first[q] + side * srows[q], srows[q])
-            left.append(ordered[micro[q], pl.ds(at, srows[q]), :])
+            g, off, n = PLAN[q]
+            at = pl.multiple_of(first[g] + side * gs[g] + off, n)
+            left.append(ordered[micro[g], pl.ds(at, n), :])
         left = jnp.concatenate(left, axis=0)
 
-        @pl.loop(0, 4)
-        def _(j):
-            cols = pl.ds(pl.multiple_of(j * (vocab // 4), vocab // 4), vocab // 4)
-            out = jnp.dot(left, weight[:, cols], preferred_element_type=F32)
-            target[:, cols] = out
-
-    def pair_copy(q):
-        return pltpu.make_async_remote_copy(
-            src_ref=sent.at[pl.ds(base[q], srows[q])],
-            dst_ref=got.at[pl.ds(base[q], srows[q])],
-            send_sem=pair_send.at[q],
-            recv_sem=pair_recv.at[q],
-            device_id=pair,
-            device_id_type=MESH,
-        )
+        for j in range(4):
+            cols = pl.ds(j * (vocab // 4), vocab // 4)
+            target[:, cols] = jnp.dot(left, weight[:, cols], preferred_element_type=F32)
+
+    def pair_copies(q):
+        parts = 2 if q == 0 else 1
+        wide = vocab // parts
+        copies = []
+        for p in range(parts):
+            at = (pl.ds(base[q], srows[q]), pl.ds(p * wide, wide))
+            sem = chunks if p else q
+            copies.append(
+                pltpu.make_async_remote_copy(
+                    src_ref=sent.at[at],
+                    dst_ref=got.at[at],
+                    send_sem=pair_send.at[sem],
+                    recv_sem=pair_recv.at[sem],
+                    device_id=pair,
+                    device_id_type=MESH,
+                )
+            )
+        return copies
 
     def send(r, src, dst, send_sem, recv_sem):
         pltpu.make_async_remote_copy(
@@ -162,13 +174,17 @@
         rn, cg, per = rows_n[q], cgs[q], cols_n[q] // 4
         at = pl.ds(base[q], srows[q])
 
-        @pl.loop(0, 4)
-        def _(j):
-            cols = pl.ds(pl.multiple_of(j * (vocab // 4), vocab // 4), vocab // 4)
-            both = (mine[at, cols] + got[at, cols]).astype(BF16)
-            for i in range(per):
-                piece = both[:, i * cg : (i + 1) * cg].reshape(rn, TALL, cg)
-                logits[q][pl.ds((j * per + i) * rn, rn)] = piece
+        copies = pair_copies(q)
+        for p, copy in enumerate(copies):
+            copy.wait_recv()
+
+            @pl.loop(p * 4 // len(copies), (p + 1) * 4 // len(copies))
+            def _(j):
+                cols = pl.ds(pl.multiple_of(j * (vocab // 4), vocab // 4), vocab // 4)
+                both = (mine[at, cols] + got[at, cols]).astype(BF16)
+                for i in range(per):
+                    piece = both[:, i * cg : (i + 1) * cg].reshape(rn, TALL, cg)
+                    logits[q][pl.ds((j * per + i) * rn, rn)] = piece
 
         @pl.loop(1, count)
         def _(k):
@@ -201,7 +217,7 @@
         pool, batch = pools[q], 8
 
         def differ(r):
-            own, other = pool[r], pool[partner[micro[q], r]]
+            own, other = pool[r], pool[partner[micro[PLAN[q][0]], r]]
             spread[q][r] = (SCALE * (own.astype(F32) - other.astype(F32))).astype(BF16)
 
         @pl.loop(0, count // batch)
@@ -281,35 +297,38 @@
         few = ref.at[pl.ds(0, ref.shape[0] - 1)]
         pltpu.make_async_copy(few, few, sem).wait()
 
-    def state_part(q):
-        lhs = jnp.concatenate(
-            [
-                grad[q][core, pl.ds(j * rows_n[q], rows_n[q])].reshape(srows[q], cgs[q])
-                for j in range(cols_n[q])
-            ],
-            axis=1,
-        )
+    def state_part(g):
+        lhs = [
+            jnp.concatenate(
+                [
+                    grad[q][core, pl.ds(j * rows_n[q], rows_n[q])].reshape(srows[q], cgs[q])
+                    for j in range(cols_n[q])
+                ],
+                axis=1,
+            )
+            for q in of[g]
+        ]
+        lhs = jnp.concatenate(lhs, axis=0)
         for w in range(2):
             out = jnp.dot(lhs, weight_t[w], preferred_element_type=F32)
-            part[q][w] = out
-            part_b[q][:, w] = out.reshape(NX, quarter[q], width).astype(BF16)
+            part[g][w] = out
+            part_b[g][:, w] = out.reshape(NX, quarter[g], width).astype(BF16)
 
     def head():
-        wide = vocab // 8
-        for j in range(8):
+        parts = min(8, min(cols_n))
+        wide = vocab // parts
+        for j in range(parts):
             cols = pl.ds(j * wide, wide)
             right = []
-            for q in range(chunks):
-                per, rn = cols_n[q] // 8, rows_n[q]
-                right.append(
-                    jnp.concatenate(
-                        [
-                            grad[q][:, pl.ds((j * per + i) * rn, rn)].reshape(2 * srows[q], cgs[q])
+            for g in range(groups):
+                for side in range(2):
+                    for q in of[g]:
+                        per, rn = cols_n[q] // parts, rows_n[q]
+                        pieces = [
+                            grad[q][side, pl.ds((j * per + i) * rn, rn)].reshape(srows[q], cgs[q])
                             for i in range(per)
-                        ],
-                        axis=1,
-                    )
-                )
+                        ]
+                        right.append(jnp.concatenate(pieces, axis=1))
             right = jnp.concatenate(right, axis=0)
             out = jnp.dot(ordered_t[...], right, preferred_element_type=F32)
             head_out[:, cols] = out.astype(BF16)
@@ -326,9 +345,9 @@
 
     def restore(m):
         rows_of = [
-            total[q][...].astype(F32).reshape(2 * srows[q], width).astype(BF16)
-            for q in range(chunks)
-            if micro[q] == m
+            total[g][...].astype(F32).reshape(2 * gs[g], width).astype(BF16)
+            for g in range(groups)
+            if micro[g] == m
         ]
         state_out[m] = lax.dot_general(
             onehot[m],
@@ -372,10 +391,9 @@
     with scope("barrier"):
         pl.semaphore_wait(barrier, count - 1 + 1 + 2 * (NX - 1) + 1)
     for q in range(chunks):
-        pair_copy(q).start()
+        for copy in pair_copies(q):
+            copy.start()
     for q in range(chunks):
-        with scope(f"pairwait{q}"):
-            pair_copy(q).wait_recv()
         with scope(f"settle{q}"):
             settle(q)
     with scope("turn"):
@@ -389,44 +407,47 @@
         with scope(f"compare{q}"):
             compare(q)
     turned().wait_recv()
-    for q in range(chunks):
-        with scope(f"wait2_{q}"):
-            await_ref(grad[q].at[core], two_recv.at[q])
-        forward(q).start()
-        with scope(f"state_part{q}"):
-            state_part(q)
+    for g in range(groups):
+        for q in of[g]:
+            with scope(f"wait2_{q}"):
+                await_ref(grad[q].at[core], two_recv.at[q])
+            forward(q).start()
+        with scope(f"state_part{g}"):
+            state_part(g)
         for k in sorted(range(1, NX), key=lambda k: -min(k, NX - k)):
-            scatter(q, k).start()
-        if q > 0:
-            x_stage(q - 1)
-        if q > 2:
-            y_stage(q - 3)
-    x_stage(chunks - 1)
-    y_stage(chunks - 3)
+            scatter(g, k).start()
+        if g > 0:
+            x_stage(g - 1)
+        if g > 2:
+            y_stage(g - 3)
+    x_stage(groups - 1)
+    y_stage(groups - 3)
     with scope("fwd_wait"):
         for q in range(chunks):
             forward(q).wait_recv()
     with scope("head"):
         head()
-    y_stage(chunks - 2)
-    y_stage(chunks - 1)
+    y_stage(groups - 2)
+    y_stage(groups - 1)
     for m in range(mb):
-        for q in range(chunks):
-            if micro[q] == m:
-                done(q)
+        for g in range(groups):
+            if micro[g] == m:
+                done(g)
         with scope(f"restore{m}"):
             restore(m)
 
     with scope("drain"):
         turned().wait_send()
         for q in range(chunks):
-            pair_copy(q).wait_send()
+            for copy in pair_copies(q):
+                copy.wait_send()
             others(logits[q], one_send.at[q])
             others(spread[q], two_send.at[q])
             forward(q).wait_send()
-            others(part_b[q], xs_send.at[q])
-            others(total[q], xg_send.at[q])
-            cross(q).wait_send()
+        for g in range(groups):
+            others(part_b[g], xs_send.at[g])
+            others(total[g], xg_send.at[g])
+            cross(g).wait_send()
         pltpu.make_async_copy(head_out, head_hbm, out_sem.at[0]).wait()
         pltpu.make_async_copy(state_out, state_hbm, out_sem.at[1]).wait()
 
@@ -459,9 +480,11 @@
         vocab = head_weight.shape[1]
         count = NZ * NY
         chunks = len(PLAN)
-        srows = [n for _, n in PLAN]
+        groups = len(GROUPS)
+        srows = [n for _, _, n in PLAN]
+        gs = [sum(ns) for _, ns in GROUPS]
         slots = [(count, TALL, vocab * n // (count * TALL)) for n in srows]
-        quarter = [n // NX for n in srows]
+        quarter = [n // NX for n in gs]
         vm = pltpu.VMEM
         dma = pltpu.SemaphoreType.DMA
         hbm = pl.BlockSpec(memory_space=pl.ANY)
@@ -490,7 +513,7 @@
                 [vm(slot, BF16) for slot in slots],
                 [vm(slot, BF16) for slot in slots],
                 [vm((2, *slot), BF16) for slot in slots],
-                [vm((2, n, width), F32) for n in srows],
+                [vm((2, n, width), F32) for n in gs],
                 [vm((NX, 2, n, width), BF16) for n in quarter],
                 [vm((NX, 2, n, width), BF16) for n in quarter],
                 [vm((2, n, width), BF16) for n in quarter],
@@ -503,9 +526,10 @@
                 dma((4,)),
                 dma((2,)),
             ]
-            + [dma((chunks,))] * 8
+            + [dma((chunks + 1,))] * 2
+            + [dma((chunks,))] * 6
             + [dma((2,))]
-            + [dma((chunks,))] * 6,
+            + [dma((groups,))] * 6,
             compiler_params=pltpu.CompilerParams(
                 collective_id=0, has_side_effects=True, vmem_limit_bytes=60 * 1024 * 1024
             ),

time: 84.5 us -> 83.6 us (0.989)
  Pallas kernels: 83.7 us -> 82.8 us
where the time goes in v4:
time: 83.6 us; the launch traced here: 83.5 us
  Pallas kernels  82.8 us (99%)
    pallas_call x1, Pallas kernels, body(): pl.pallas_call(functools.partial(kernel, dims), out_shape=shapes, in_spec...  80.5 us
    pallas_call x1, Pallas kernels, body(): pl.pallas_call(finish, out_shape=shapes, in_specs=[hbm, hbm], out_specs=(...  2.36 us

profile of v4, /device:TPU:1, one launch (start us, length us, event | category | flops | bytes accessed | tf_op | source)
XLA Modules:
  0.0 83.5 jit_solution(6905961853226357986)
XLA Ops:
  0.6 80.5 %shard_map.59 = (bf16[2,256,384]{2,1,0:T(8,128)(2,1)}, bf16[384,2048]{1,0:T(8,128)(2,1)}) custom-call(s32[2,32]{1,0:T(2,128)} %order_hbm.1, bf16[2,256,384]{2,1,0:T(8,128)(2,1)} %states_hbm.1, bf16[384,2048]{1,0:T(8,128)(2,1)} %weight_hbm.1, s32[2,32,256]{2,1,0:T(8,128)} %example_hbm.1), custom_call_target="tpu_custom_call" | custom-call | tf_op jit(solution)/shard_map/pallas_call | solution.py:495
  81.1 2.4 %shard_map.60 = (bf16[2,256,384]{2,1,0:T(8,128)(2,1)}, bf16[384,2048]{1,0:T(8,128)(2,1)}) custom-call(bf16[2,256,384]{2,1,0:T(8,128)(2,1)} %get-tuple-element.4.state_in, bf16[384,2048]{1,0:T(8,128)(2,1)} %get-tuple-element.5.head_in), custom_call_target="tpu_custom_call" | custom-call | tf_op jit(solution)/shard_map/pallas_call | solution.py:538

commit v5 on v4

--- a/solution.py
+++ b/solution.py
@@ -178,9 +178,8 @@
         for p, copy in enumerate(copies):
             copy.wait_recv()
 
-            @pl.loop(p * 4 // len(copies), (p + 1) * 4 // len(copies))
-            def _(j):
-                cols = pl.ds(pl.multiple_of(j * (vocab // 4), vocab // 4), vocab // 4)
+            for j in range(p * 4 // len(copies), (p + 1) * 4 // len(copies)):
+                cols = pl.ds(j * (vocab // 4), vocab // 4)
                 both = (mine[at, cols] + got[at, cols]).astype(BF16)
                 for i in range(per):
                     piece = both[:, i * cg : (i + 1) * cg].reshape(rn, TALL, cg)

time: 83.6 us -> 82.8 us (level)
  no operation moved by 1% of the time
where the time goes in v5:
time: 82.8 us; the launch traced here: 82.7 us
  Pallas kernels  82 us (99%)
    pallas_call x1, Pallas kernels, body(): pl.pallas_call(functools.partial(kernel, dims), out_shape=shapes, in_spec...  79.7 us
    pallas_call x1, Pallas kernels, body(): pl.pallas_call(finish, out_shape=shapes, in_specs=[hbm, hbm], out_specs=(...  2.36 us

profile of v5, /device:TPU:1, one launch (start us, length us, event | category | flops | bytes accessed | tf_op | source)
XLA Modules:
  0.0 82.7 jit_solution(13777548459715783590)
XLA Ops:
  0.6 79.7 %shard_map.59 = (bf16[2,256,384]{2,1,0:T(8,128)(2,1)}, bf16[384,2048]{1,0:T(8,128)(2,1)}) custom-call(s32[2,32]{1,0:T(2,128)} %order_hbm.1, bf16[2,256,384]{2,1,0:T(8,128)(2,1)} %states_hbm.1, bf16[384,2048]{1,0:T(8,128)(2,1)} %weight_hbm.1, s32[2,32,256]{2,1,0:T(8,128)} %example_hbm.1), custom_call_target="tpu_custom_call" | custom-call | tf_op jit(solution)/shard_map/pallas_call | solution.py:494
  80.3 2.4 %shard_map.60 = (bf16[2,256,384]{2,1,0:T(8,128)(2,1)}, bf16[384,2048]{1,0:T(8,128)(2,1)}) custom-call(bf16[2,256,384]{2,1,0:T(8,128)(2,1)} %get-tuple-element.4.state_in, bf16[384,2048]{1,0:T(8,128)(2,1)} %get-tuple-element.5.head_in), custom_call_target="tpu_custom_call" | custom-call | tf_op jit(solution)/shard_map/pallas_call | solution.py:537
